TPU v7x, 512 devices: a whole 4x4x16 slice. The times are simulated.
512 devices in a mesh: row: 16 (over x, z_hi, core), col: 32 (over y, z_lo).
Axes of the slice: x: 4, y: 4, z: 16 (z_hi: 2, z_lo: 8; z = z_hi * 8 + z_lo), core: 2. Of those that a mesh axis runs over, the one named last changes fastest.
Arguments:
- a_blocks: float32 [384, 16, 128, 128], P('col', 'row'), may hold values from -0.25 to 0.25
- a_cols: int32 [384, 16], P('col'), may hold values from 0 to 63, as said below
- a_lengths: int32 [384], P('col'), may hold values from 1 to 16, as said below
- b_blocks: float32 [64, 16, 128, 128], P('col', 'row'), may hold values from -6 to 6
- b_cols: int32 [64, 16], P(None, 'row'), may hold values from 0 to 7
- c_cols: int32 [384, 64], P('col', 'row'), may hold values from 0 to 7, as said below
- order: int32 [64], replicated, may hold values from 0 to 63, each once
Outputs:
- c_blocks: float32 [384, 64, 128, 128], P('col', 'row')
Inputs may be any that keep to these rules, and one draw needn't show every extreme that they name: `a_cols`: the 16 entries of one row are distinct. `a_lengths`: the first row has 16 live slots; slots at or after a row's length hold blocks that are not used. `c_cols`: the 4 entries of one row in one row group are distinct. `order`: each number once.
All inputs are finite; a program needn't handle non-finite values.
Results may differ from a plain program's by a relative error of at most 0.0003.
Values sent between devices are 32-bit elements; how exact they have to be, the bound alone decides.
No kernel may reach another device: no remote copies, remote signals or barrier semaphores. Data moves between devices by JAX's collectives and lax.ppermute only.
A program may use at most 64 MiB of HBM per device.

v0:
```python
import jax
import jax.numpy as jnp
from jax import lax
from jax.sharding import PartitionSpec as P


def lookup(values_table, indices):
    matched = indices[..., None] == jnp.arange(values_table.shape[0], dtype=jnp.int32)
    return jnp.sum(jnp.where(matched, values_table, 0), axis=-1)


def local(a_blocks, a_cols, a_lengths, b_blocks, b_cols, c_cols, order):
    panels = lax.all_gather(b_blocks, "col", axis=0, tiled=True)[:, 0]
    rows_here, slot_all = a_cols.shape
    pattern_slots = c_cols.shape[1]
    block_size = panels.shape[-1]
    position = lookup(order, a_cols)
    window_col = lookup(b_cols[:, 0], position)
    live_slots = jnp.arange(slot_all, dtype=jnp.int32)[None, :] < a_lengths[:, None]
    weights = ((window_col[:, :, None] == c_cols[:, None, :]) & live_slots[:, :, None]).astype(
        jnp.float32
    )
    zero_sums = jnp.zeros((rows_here, pattern_slots, block_size, block_size), jnp.float32)
    whole_slots = lax.all_gather(a_blocks, "row", axis=1, tiled=True)

    def per_row(row_index, running):
        chosen = jnp.take(panels, position[row_index], axis=0)
        products = jnp.einsum(
            "jab,jbc->jac", whole_slots[row_index], chosen, precision=lax.Precision.HIGHEST
        )
        landed = jnp.einsum(
            "js,jac->sac", weights[row_index], products, precision=lax.Precision.HIGHEST
        )
        return running.at[row_index].add(landed)

    return lax.fori_loop(0, rows_here, per_row, zero_sums)


def solution(mesh):
    return jax.shard_map(
        local,
        mesh=mesh,
        in_specs=(
            P("col", "row", None, None),
            P("col", None),
            P("col"),
            P("col", "row", None, None),
            P(None, "row"),
            P("col", "row"),
            P(),
        ),
        out_specs=P("col", "row", None, None),
        check_vma=False,
    )
```

profile of v0, /device:TPU:105, one launch (start us, length us, event | category | flops | bytes accessed | tf_op | source)
XLA Modules:
  0.0 615.6 jit_solution(10681453512464985414)
XLA Ops:
  11.7 190.3 %all-gather.5.cloned.1.call-done = f32[64,1,128,128]{3,2,1,0:T(8,128)} async-done(((f32[2,1,128,128]{3,2,1,0:T(8,128)}), f32[64,1,128,128]{3,2,1,0:T(8,128)}) %all-gather.5.cloned.1.call-update) | async-done | bytes 4194320 | tf_op jit(solution)/shard_map/all_gather | solution.py:13
  202.0 290.2 %all-gather.3.cloned.1.call-done = f32[12,16,128,128]{3,2,1,0:T(8,128)} async-done(((f32[12,1,128,128]{3,2,1,0:T(8,128)}), f32[12,16,128,128]{3,2,1,0:T(8,128)}) %all-gather.3.cloned.1.call-update) | async-done | bytes 12582928 | tf_op jit(solution)/shard_map/all_gather | solution.py:24
  494.3 114.5 %while.14 = (s32[]{:T(128)}, f32[12,4,128,128]{3,2,1,0:T(8,128)}, f32[12,16,4]{1,2,0:T(4,128)S(1)}, f32[12,16,128,128]{3,2,1,0:T(8,128)}, s32[12,16]{1,0:T(8,128...) while((s32[]{:T(128)}, f32[12,4,128,128]{3,2,1,0:T(8,128)}, ...), condition=%wide.region_4.5_spmd, body=%wide.region_2.4_spmd.sunk | while | flops 415630528 | bytes 7871975 | solution.py:36
  494.3 2.8 gather_fusion
  497.1 2.4 fusion.27
  503.8 2.8 gather_fusion
  506.7 2.4 fusion.27
  513.4 2.8 gather_fusion
  522.9 2.8 gather_fusion
  525.7 2.4 fusion.27
  532.5 2.8 gather_fusion
  535.3 2.4 fusion.27
  542.0 2.8 gather_fusion
  544.8 2.4 fusion.27
  551.5 2.8 gather_fusion
  554.4 2.4 fusion.27
  561.1 2.8 gather_fusion
  570.6 2.8 gather_fusion
  573.4 2.4 fusion.27
  580.2 2.8 gather_fusion
  583.0 2.4 fusion.27
  589.7 2.8 gather_fusion
  592.5 2.4 fusion.27
  599.2 2.8 gather_fusion
  (99 shorter events, 65.8 us)
Async XLA Ops:
  6.5 487.7 %copy-start = (s32[4]{0:T(128)S(1)}, s32[4]{0:T(128)}, u32[]{:S(2)}) copy-start(s32[4]{0:T(128)} %constant.90.clone.1) | copy-start | bytes 52
  6.5 195.5 %all-gather.5.cloned.1.call-start = ((), (), s32[]{:S(2)}) async-start(), calls=%async_computation.1 | async-start | bytes 4325376 | tf_op jit(solution)/shard_map/all_gather | solution.py:13
  7.3 485.0 %all-gather.3.cloned.1.call-start = ((), (), s32[]{:S(2)}) async-start(), calls=%async_computation | async-start | bytes 13369344 | tf_op jit(solution)/shard_map/all_gather | solution.py:24
Sparse Core Ops, SparseCore 0:
  9.4 192.5 all-gather.4
  205.3 286.8 all-gather.2
where the time goes:
time: 617 us; the launch traced here: 616 us
  waiting for transfers between devices  482 us (78%)
  local copies, waits for them, and re-layouts  56.7 us (9%)
  matrix products  51.2 us (8%)
  between operations  13.4 us (2%)
  other arithmetic  11.8 us (2%)
    all_gather x1, waiting for transfers between devices, local(): whole_slots = lax.all_gather(a_blocks, 'row', axis=1, tiled=True)  290 us
    all_gather x1, waiting for transfers between devices, local(): panels = lax.all_gather(b_blocks, 'col', axis=0, tiled=True)[:, 0]  190 us
    gather x12, local copies, waits for them, and re-layouts, per_row(): chosen = jnp.take(panels, position[row_index], axis=0)  33.6 us
    dot_general x12, matrix products, per_row(): jnp.einsum('jab,jbc->jac', whole_slots[row_index], chosen, precision=lax....  29.1 us
    dot_general x12, matrix products, per_row(): jnp.einsum('js,jac->sac', weights[row_index], products, precision=lax.Pre...  22.2 us
  transfers between devices with their start and end apart: 2, of which 2 were waited for; matrix products, arithmetic and copies ran while one was open for 1% of the time, Pallas kernels for 0%

commit v1 on v0

--- a/solution.py
+++ b/solution.py
@@ -2,6 +2,14 @@
 import jax.numpy as jnp
 from jax import lax
 from jax.sharding import PartitionSpec as P
+
+
+def review_the_quotas(x_part, mesh_ax="row"):
+    y2 = jax.lax.axis_size(mesh_ax)
+    oldest = jax.lax.all_to_all(
+        jnp.stack([x_part] * y2, 0), axis_name=mesh_ax, split_axis=0, concat_axis=0
+    )
+    return jnp.concatenate(oldest, axis=1)
 
 
 def lookup(values_table, indices):
@@ -21,7 +29,7 @@
         jnp.float32
     )
     zero_sums = jnp.zeros((rows_here, pattern_slots, block_size, block_size), jnp.float32)
-    whole_slots = lax.all_gather(a_blocks, "row", axis=1, tiled=True)
+    whole_slots = review_the_quotas(a_blocks)
 
     def per_row(row_index, running):
         chosen = jnp.take(panels, position[row_index], axis=0)

time: 617 us -> 800 us (1.30)
  the two profiles are of different devices: /device:TPU:105 before, /device:TPU:98 now
where the time goes in v1:
time: 800 us; the launch traced here: 798 us
  waiting for transfers between devices  643 us (80%)
  local copies, waits for them, and re-layouts  63.3 us (8%)
  matrix products  52.1 us (7%)
  starting transfers between devices  15.6 us (2%)
  between operations  13.5 us (2%)
  other arithmetic  10.2 us (1%)
    all_gather x1, waiting for transfers between devices, local(): panels = lax.all_gather(b_blocks, 'col', axis=0, tiled=True)[:, 0]  342 us
    all_to_all x1, waiting for transfers between devices, review_the_quotas(): jax.lax.all_to_all(jnp.stack([x_part] * y2, 0), axis_name=mesh_ax, split_...  301 us
    gather x12, local copies, waits for them, and re-layouts, per_row(): chosen = jnp.take(panels, position[row_index], axis=0)  33.6 us
    dot_general x12, matrix products, per_row(): jnp.einsum('jab,jbc->jac', whole_slots[row_index], chosen, precision=lax....  29.1 us
    dot_general x12, matrix products, per_row(): jnp.einsum('js,jac->sac', weights[row_index], products, precision=lax.Pre...  23 us
  transfers between devices with their start and end apart: 2, of which 2 were waited for; matrix products, arithmetic and copies ran while one was open for 0% of the time, Pallas kernels for 0%

profile of v1, /device:TPU:98, one launch (start us, length us, event | category | flops | bytes accessed | tf_op | source)
XLA Modules:
  0.0 798.4 jit_solution(12758399397996000306)
XLA Ops:
  6.5 7.2 stack.2
  13.7 15.5 %all-to-all-start = ((f32[16,12,1,128,128]{4,3,1,2,0:T(8,128)}), f32[16,12,1,128,128]{4,3,1,2,0:T(8,128)}, u32[]{:S(2)}, u32[]{:S(2)}) async-start(f32[16,12,1,128,128]{4,3,1,2,0:T(8,128)} %stack.2), calls=%async_computation | async-start | bytes 25165824 | tf_op jit(solution)/shard_map/all_to_all | solution.py:9
  31.0 342.0 %all-gather.2.cloned.1.call-done = f32[64,1,128,128]{3,2,1,0:T(8,128)} async-done(((f32[2,1,128,128]{3,2,1,0:T(8,128)}), f32[64,1,128,128]{3,2,1,0:T(8,128)}) %all-gather.2.cloned.1.call-update) | async-done | bytes 4194320 | tf_op jit(solution)/shard_map/all_gather | solution.py:21
  373.0 300.7 %all-to-all-done = f32[16,12,1,128,128]{4,3,1,2,0:T(8,128)} async-done(((f32[16,12,1,128,128]{4,3,1,2,0:T(8,128)}), f32[16,12,1,128,128]{4,3,1,2,0:T(8,128)}, u32[]{:S(2)}, u32[]{:S(2)}) %all-to-all-start) | async-done | bytes 12582944 | tf_op jit(solution)/shard_map/all_to_all | solution.py:9
  675.7 115.8 %while.14 = (s32[]{:T(128)}, f32[12,4,128,128]{3,2,1,0:T(8,128)}, f32[12,16,4]{1,2,0:T(4,128)S(1)}, f32[12,16,128,128]{3,2,0,1:T(8,128)}, s32[12,16]{1,0:T(8,128...) while((s32[]{:T(128)}, f32[12,4,128,128]{3,2,1,0:T(8,128)}, ...), condition=%wide.region_4.5_spmd, body=%wide.region_2.4_spmd.sunk | while | flops 415630528 | bytes 7871975 | solution.py:44
  675.8 2.8 gather_fusion
  678.6 2.4 fusion.27
  685.4 2.8 gather_fusion
  688.3 2.4 fusion.27
  695.1 2.8 gather_fusion
  697.9 2.4 fusion.27
  704.7 2.8 gather_fusion
  707.6 2.4 fusion.27
  714.4 2.8 gather_fusion
  717.2 2.4 fusion.27
  724.0 2.8 gather_fusion
  726.9 2.4 fusion.27
  733.7 2.8 gather_fusion
  736.5 2.4 fusion.27
  743.3 2.8 gather_fusion
  753.0 2.8 gather_fusion
  762.6 2.8 gather_fusion
  772.3 2.8 gather_fusion
  781.9 2.8 gather_fusion
  (109 shorter events, 68.5 us)
Async XLA Ops:
  13.7 16.3 %copy-start.2 = (s32[12,4]{0,1:T(4,128)S(1)}, s32[12,4]{0,1:T(4,128)}, u32[]{:S(2)}) copy-start(s32[12,4]{0,1:T(4,128)} %param.16) | copy-start | bytes 580
  13.7 16.4 %copy-start.1 = (s32[12,16]{1,0:T(8,128)S(1)}, s32[12,16]{1,0:T(8,128)}, u32[]{:S(2)}) copy-start(s32[12,16]{1,0:T(8,128)} %param.12) | copy-start | bytes 2308
  13.7 16.4 %copy-start.3 = (s32[64]{0:T(128)S(1)}, s32[64]{0:T(128)}, u32[]{:S(2)}) copy-start(s32[64]{0:T(128)} %param.17) | copy-start | bytes 772
  13.7 16.8 %copy-start.4 = (s32[64,1]{0,1:T(1,128)S(1)}, s32[64,1]{0,1:T(1,128)}, u32[]{:S(2)}) copy-start(s32[64,1]{0,1:T(1,128)} %param.15) | copy-start | bytes 772
  13.7 17.1 %copy-start.5 = (s32[12]{0:T(128)S(1)}, s32[12]{0:T(128)}, u32[]{:S(2)}) copy-start(s32[12]{0:T(128)} %param.13) | copy-start | bytes 148
  13.7 660.0 %all-to-all-start = ((f32[16,12,1,128,128]{4,3,1,2,0:T(8,128)}), f32[16,12,1,128,128]{4,3,1,2,0:T(8,128)}, u32[]{:S(2)}, u32[]{:S(2)}) async-start(f32[16,12,1,128,128]{4,3,1,2,0:T(8,128)} %stack.2), calls=%async_computation | async-start | bytes 25165824 | tf_op jit(solution)/shard_map/all_to_all | solution.py:9
  29.3 646.5 %copy-start = (s32[4]{0:T(128)S(1)}, s32[4]{0:T(128)}, u32[]{:S(2)}) copy-start(s32[4]{0:T(128)} %constant.90.clone.1) | copy-start | bytes 52
  29.3 343.7 %all-gather.2.cloned.1.call-start = ((), (), s32[]{:S(2)}) async-start(), calls=%async_computation.1 | async-start | bytes 4325376 | tf_op jit(solution)/shard_map/all_gather | solution.py:21
Sparse Core Ops, SparseCore 0:
  32.2 340.7 all-gather.1
